TPU v7x, 32 devices: a whole 2x2x4 slice. The times are simulated.
32 devices in a mesh: slab: 8 (over z, y), tile: 4 (over x, core).
Axes of the slice: x: 2, y: 2, z: 4, core: 2. Of those that a mesh axis runs over, the one named last changes fastest.
Arguments:
- grid: bfloat16 [64, 256, 1024], P('slab', 'tile'), may hold values from -6 to 6
- type_table: float32 [16, 8], replicated, may hold values from -4 to 4
- counts: int32 [512], P(('slab', 'tile')), may hold values from 10 to 120
- types: int32 [512, 128], P(('slab', 'tile')), may hold values from 0 to 15
- offsets: float32 [512, 3, 128], P(('slab', 'tile')), may hold values from 0 to 0.999
- route: int32 [512, 1], P('slab'), may hold values from 0 to 7; in each aligned block of 64 rows (0 to 63, 64 to 127, ...) at most 16 rows name the same one
- base_y: int32 [512], P(('slab', 'tile')), may hold values from 0 to 223
- base_z: int32 [512], P(('slab', 'tile')), may hold values from 0 to 95
Outputs:
- energy: float32 [512], P(('slab', 'tile'))
Inputs may be any that keep to these rules, and one draw needn't show every extreme that they name: `route`: among the rows of one aligned block of 64 poses (those starting on one group of tile devices), at most 16 name the same slab.
All inputs are finite; a program needn't handle non-finite values.
Results may differ from a plain program's by a relative error of at most 0.0003.
Values may be sent and summed in bfloat16 or wider, within the bound.
A program may use at most 64 MiB of HBM per device.

v0:
```python
import jax
import jax.numpy as jnp
from jax import lax
from jax.sharding import PartitionSpec as P

SPAN = 32


def from_behind(shard, axis, by):
    devices = lax.axis_size(axis)
    pairs = [(i, i + by) for i in range(devices) if 0 <= i + by < devices]
    return lax.ppermute(shard, axis, pairs)


def build_payload(type_table, counts, types, offsets, base_y, base_z, cells_x):
    atom_slots = types.shape[1]
    onehot = (types[:, :, None] == jnp.arange(type_table.shape[0])[None, None, :]).astype(
        jnp.float32
    )
    typed = jnp.einsum("pat,tc->pca", onehot, type_table, precision=lax.Precision.HIGHEST)
    live = (jnp.arange(atom_slots)[None, :] < counts[:, None]).astype(jnp.float32) / counts[
        :, None
    ].astype(jnp.float32)
    coef = typed * live[:, None, :]
    local_x = offsets[:, 0, :] * (cells_x - 1)
    pos_y = base_y[:, None].astype(jnp.float32) + offsets[:, 1, :] * SPAN
    pos_z = base_z[:, None].astype(jnp.float32) + offsets[:, 2, :] * SPAN
    return jnp.concatenate(
        [local_x[:, None, :], pos_y[:, None, :], pos_z[:, None, :], coef], axis=1
    )


def slot_ranks(targets):
    count = targets.shape[0]
    order = jnp.arange(count)
    same = (targets[:, None] == targets[None, :]) & (order[:, None] > order[None, :])
    return jnp.sum(same.astype(jnp.int32), axis=1)


def slot_table(targets, ranks, slabs, slots):
    count = targets.shape[0]
    hits = (
        (targets[None, None, :] == jnp.arange(slabs)[:, None, None])
        & (ranks[None, None, :] == jnp.arange(slots)[None, :, None])
    ).astype(jnp.int32)
    owner = jnp.sum(hits * jnp.arange(count)[None, None, :], axis=2)
    filled = jnp.sum(hits, axis=2)
    return (owner.reshape(-1), filled.reshape(-1))


def corner_table(grid, rim, cells_x, cells_y, cells_z, chans):
    extended = jnp.concatenate([grid, rim], axis=1).reshape(cells_x, cells_y + 1, cells_z, chans)
    paired = jnp.concatenate([extended[:, :, :-1, :], extended[:, :, 1:, :]], axis=3)
    square = jnp.concatenate([paired[:, :-1], paired[:, 1:]], axis=3)
    return square.reshape(cells_x * cells_y * (cells_z - 1), 4 * chans)


def score(slots_data, table, tile_index, cells_x, cells_y, cells_z, chans):
    local_x = slots_data[:, 0, :]
    local_y = slots_data[:, 1, :] - (tile_index * cells_y).astype(jnp.float32)
    pos_z = slots_data[:, 2, :]
    coef = jnp.swapaxes(slots_data[:, 3:, :], 1, 2)
    floor_x = jnp.floor(local_x)
    floor_y = jnp.floor(local_y)
    floor_z = jnp.floor(pos_z)
    inside = ((floor_y >= 0) & (floor_y < cells_y)).astype(jnp.float32)
    cell_x = jnp.clip(floor_x, 0, cells_x - 2)
    cell_y = jnp.clip(floor_y, 0, cells_y - 1)
    cell_z = jnp.clip(floor_z, 0, cells_z - 2)
    frac_x = local_x - cell_x
    frac_y = local_y - cell_y
    frac_z = pos_z - cell_z
    int_x = cell_x.astype(jnp.int32)
    int_y = cell_y.astype(jnp.int32)
    int_z = cell_z.astype(jnp.int32)
    quarter = jnp.stack(
        [
            (1.0 - frac_y) * (1.0 - frac_z),
            (1.0 - frac_y) * frac_z,
            frac_y * (1.0 - frac_z),
            frac_y * frac_z,
        ],
        axis=2,
    )
    lines = cells_y * (cells_z - 1)
    index = int_x * lines + int_y * (cells_z - 1) + int_z
    total = jnp.zeros(local_x.shape + (chans,), jnp.float32)
    for step_x in range(2):
        factor = frac_x if step_x else 1.0 - frac_x
        values = jnp.take(table, index + step_x * lines, axis=0).astype(jnp.float32)
        values = values.reshape(local_x.shape + (4, chans))
        mixed = jnp.sum(quarter[:, :, :, None] * values, axis=2)
        total = total + factor[:, :, None] * mixed
    return jnp.sum(jnp.sum(total * coef, axis=2) * inside, axis=1)


def body(grid, type_table, counts, types, offsets, route, base_y, base_z):
    tile_index = lax.axis_index("tile")
    slabs = lax.axis_size("slab")
    pose_count = counts.shape[0]
    atom_slots = types.shape[1]
    chans = type_table.shape[1]
    cells_x, cells_y, wide_z = grid.shape
    cells_z = wide_z // chans
    capacity = max(2, 8 * pose_count // slabs)
    rim = from_behind(grid[:, :1, :], "tile", -1)
    table = corner_table(grid, rim, cells_x, cells_y, cells_z, chans)
    targets = route[:, 0]
    ranks = slot_ranks(targets)
    owner, filled = slot_table(targets, ranks, slabs, capacity)
    used = filled.astype(jnp.float32)
    payload = build_payload(type_table, counts, types, offsets, base_y, base_z, cells_x)
    rows = payload.shape[1]
    grouped = lax.all_gather(payload, "tile", axis=0, tiled=True)
    outgoing = (jnp.take(grouped, owner, axis=0) * used[:, None, None]).reshape(
        slabs, capacity, rows, atom_slots
    )
    incoming = lax.all_to_all(outgoing, "slab", split_axis=0, concat_axis=0, tiled=True)
    slots_data = incoming.reshape(slabs * capacity, rows, atom_slots)
    partial_value = score(slots_data, table, tile_index, cells_x, cells_y, cells_z, chans)
    returned = lax.all_to_all(
        partial_value.reshape(slabs, capacity), "slab", split_axis=0, concat_axis=0, tiled=True
    )
    per_pose = jnp.take(returned.reshape(-1), targets * capacity + ranks, axis=0)
    return lax.psum_scatter(per_pose, "tile", scatter_dimension=0, tiled=True)


def solution(mesh):
    in_specs = (
        P("slab", "tile", None),
        P(),
        P(("slab", "tile")),
        P(("slab", "tile"), None),
        P(("slab", "tile"), None, None),
        P("slab", None),
        P(("slab", "tile")),
        P(("slab", "tile")),
    )
    out_specs = P(("slab", "tile"))
    return jax.shard_map(body, mesh=mesh, in_specs=in_specs, out_specs=out_specs, check_vma=False)
```

profile of v0, /device:TPU:0, one launch (start us, length us, event | category | flops | bytes accessed | tf_op | source)
XLA Modules:
  0.0 230.2 jit_solution(1748385922911415029)
XLA Ops:
  0.0 0.0 copy-start
  0.0 0.0 copy-start.1
  0.0 0.9 convert_reduce_fusion
  0.9 0.7 iota_compare_fusion.5
  1.6 0.4 fusion.8
  2.0 0.1 reshape.311
  2.1 0.7 convert_element_type.63
  2.7 0.7 convert_element_type.64
  3.4 0.7 convert_element_type.66
  4.0 0.7 convert_divide_fusion
  4.8 0.8 slice_multiply_fusion
  5.6 0.0 copy-done
  5.6 0.9 fusion.3
  6.4 0.1 pad_maximum_fusion.3
  6.5 7.8 %all_gather.3 = f32[64,11,128]{2,0,1:T(8,128)S(1)} all-gather(f32[16,11,128]{2,0,1:T(8,128)S(1)} %copy.126), channel_id=1, replica_groups=mesh['slab'=8,'tile'=4] {'tile'}, dimensions={0}, use_global_device_ids=true | all-gather | bytes 450560 | tf_op jit(solution)/shard_map/all_gather | solution.py:114
  14.3 0.2 copy.127
  14.6 0.8 gather_fusion
  15.3 1.2 fusion.4
  16.5 5.8 %all-to-all-start = ((f32[8,16,11,128]{3,1,2,0:T(8,128)}), f32[8,16,11,128]{3,1,2,0:T(8,128)}, u32[]{:S(2)}, u32[]{:S(2)}) async-start(f32[8,16,11,128]{3,1,2,0:T(8,128)} %fusion.4), calls=%async_computation | async-start | bytes 1441792 | tf_op jit(solution)/shard_map/all_to_all | solution.py:118
  22.3 0.9 slice.42
  23.3 1.3 collective-permute-start
  24.6 0.0 copy-done.1
  24.6 1.8 collective-permute-done
  26.4 1.4 pad_maximum_fusion.1
  27.7 1.7 copy.131
  29.4 0.5 fusion.17
  30.0 1.0 slice_maximum_fusion
  31.0 6.2 %fusion = bf16[8,64,127,32]{1,3,2,0:T(8,128)(2,1)} fusion(bf16[8,65,127,8]{1,3,2,0:T(8,128)(2,1)S(1)} %get-tuple-element.13, bf16[8,65,127,8]{1,3,2,0:T(8,128)(2,1)S(1)} %get-tuple-element.12, bf16[8,64,127,16]{1,3,2,0:T(8,128)(2,1)S(1)} %slice_maximum_fusion), kind=kLoop, calls=%fused_computation.5 | loop fusion | flops 12484608 | bytes 8355584 | tf_op jit(solution)/shard_map/concatenate | solution.py:54
  37.2 10.0 %copy.132 = bf16[8,64,127,32]{2,1,0,3:T(8,128)(2,1)} copy(bf16[8,64,127,32]{1,3,2,0:T(8,128)(2,1)} %fusion) | data formatting | bytes 8323072 | tf_op jit(solution)/shard_map/concatenate | solution.py:54
  47.2 8.5 %reshape.314 = bf16[65024,32]{0,1:T(8,128)(2,1)} reshape(bf16[8,64,127,32]{2,1,0,3:T(8,128)(2,1)} %copy.132) | data formatting | bytes 8323072 | tf_op jit(solution)/shard_map/reshape | solution.py:55
  55.8 13.5 %copy.133 = bf16[65024,32]{1,0:T(8,128)(2,1)} copy(bf16[65024,32]{0,1:T(8,128)(2,1)} %reshape.314) | data formatting | bytes 8323072 | tf_op jit(solution)/shard_map/reshape | solution.py:55
  69.3 0.0 all-to-all-done
  69.3 1.2 copy.129
  70.5 0.1 compare_and_fusion
  70.7 0.9 copy.130
  71.6 62.9 %gather_fusion.3 = bf16[16384,32]{1,0:T(8,128)(2,1)} fusion(bf16[65024,32]{1,0:T(8,128)(2,1)} %copy.133, s32[16384]{0:T(1024)S(1)} %get-tuple-element.20), kind=kCustom, calls=%fused_computation.1.clone | custom fusion | bytes 2162688 | tf_op jit(solution)/shard_map/jit(_take)/gather | solution.py:90
  134.5 3.6 %copy.136 = bf16[128,128,32]{1,2,0:T(8,128)(2,1)S(1)} copy(bf16[128,128,32]{2,1,0:T(8,128)(2,1)} %bitcast.96) | data formatting | bytes 2097152 | tf_op jit(solution)/shard_map/jit(_take)/gather | solution.py:90
  138.1 62.9 %gather_fusion.2 = bf16[16384,32]{1,0:T(8,128)(2,1)} fusion(bf16[65024,32]{1,0:T(8,128)(2,1)} %copy.133, s32[16384]{0:T(1024)S(1)} %get-tuple-element.21), kind=kCustom, calls=%fused_computation.clone | custom fusion | bytes 2162688 | tf_op jit(solution)/shard_map/jit(_take)/gather | solution.py:90
  201.0 0.0 copy-start.2
  201.0 3.8 %copy.134 = bf16[128,128,32]{1,2,0:T(8,128)(2,1)S(1)} copy(bf16[128,128,32]{2,1,0:T(8,128)(2,1)} %bitcast.95) | data formatting | bytes 2097152 | tf_op jit(solution)/shard_map/jit(_take)/gather | solution.py:90
  204.8 2.4 %fusion.2 = (f32[128,128,8]{1,2,0:T(8,128)S(1)}, f32[128,128,8]{1,2,0:T(8,128)S(1)}) fusion(bf16[128,128,32]{1,2,0:T(8,128)(2,1)S(1)} %copy.134, f32[128,128,4]{1,2,0:T(4,128)} %copy.130, pred[128,128]{1,0:T(8,128)(4,1)S(1)} %compare_and_fusion.1, bf16[128,128,32]{1,2,0:T(8,128)(2,1)S(1)} %copy.136, pred[128,128]{1,0:T(8,128)(4,1)S(1)} %get-tuple-element.10), kind=kLoop, calls=%fused_computation.10 | loop fusion | flops 3932160 | bytes 3440640 | tf_op jit(solution)/shard_map/reduce_sum | solution.py:92
  207.2 0.6 fusion.6
  207.7 0.1 select_reduce_fusion
  207.9 0.7 all_to_all.10
  208.5 6.0 %all-to-all-start.1 = ((f32[8,1,16]{2,1,0:T(1,128)}), f32[8,1,16]{2,1,0:T(1,128)S(1)}, u32[]{:S(2)}, u32[]{:S(2)}) async-start(f32[8,1,16]{2,1,0:T(1,128)} %bitcast.25), calls=%async_computation.1 | async-start | bytes 8192 | tf_op jit(solution)/shard_map/all_to_all | solution.py:121
  214.5 0.0 copy-done.2
  214.6 0.6 dynamic-slice
  215.8 5.2 %all-to-all-done.1 = f32[8,1,16]{2,1,0:T(1,128)S(1)} async-done(((f32[8,1,16]{2,1,0:T(1,128)}), f32[8,1,16]{2,1,0:T(1,128)S(1)}, u32[]{:S(2)}, u32[]{:S(2)}) %all-to-all-start.1) | async-done | bytes 544 | tf_op jit(solution)/shard_map/all_to_all | solution.py:121
  221.0 0.5 broadcast.308
  221.5 0.7 reduce.3
  222.2 0.1 reshape.319
  222.3 0.8 gather_fusion.1
  223.1 6.5 %all-reduce = f32[64]{0:T(128)S(1)} all-reduce(f32[64]{0:T(128)S(1)} %bitcast_select_fusion), channel_id=2, replica_groups=mesh['slab'=8,'tile'=4] {'tile'}, use_global_device_ids=true, to_apply=%region_7.9.clone | all-reduce | flops 64 | bytes 512
  229.6 0.6 dynamic-slice.1
  (15 shorter events, 0.2 us)
Async XLA Ops:
  0.0 5.6 %copy-start = (f32[16,8]{0,1:T(8,128)S(1)}, f32[16,8]{0,1:T(8,128)}, u32[]{:S(2)}) copy-start(f32[16,8]{0,1:T(8,128)} %param.11) | copy-start | bytes 1540
  0.0 24.6 %copy-start.1 = (s32[64,1]{0,1:T(1,128)S(1)}, s32[64,1]{0,1:T(1,128)}, u32[]{:S(2)}) copy-start(s32[64,1]{0,1:T(1,128)} %param.15) | copy-start | bytes 772
  16.5 52.8 %all-to-all-start = ((f32[8,16,11,128]{3,1,2,0:T(8,128)}), f32[8,16,11,128]{3,1,2,0:T(8,128)}, u32[]{:S(2)}, u32[]{:S(2)}) async-start(f32[8,16,11,128]{3,1,2,0:T(8,128)} %fusion.4), calls=%async_computation | async-start | bytes 1441792 | tf_op jit(solution)/shard_map/all_to_all | solution.py:118
  23.3 3.1 %collective-permute-start = (bf16[8,1,1024]{2,1,0:T(2,128)(2,1)S(1)}, bf16[8,1,1024]{2,1,0:T(2,128)(2,1)S(1)}, u32[]{:S(2)}, u32[]{:S(2)}) collective-permute-start(bf16[8,1,1024]{2,1,0:T(2,128)(2,1)S(1)} %slice.42), channel_id=1, source_target_pairs={{1,0},{2,1},{3,2},{5,4},{6,5},{7,6},{9,8},{10,9},{11,10},{13,12},{... | collective-permute-start | bytes 49160 | tf_op jit(solution)/shard_map/ppermute | solution.py:12
  201.0 13.5 %copy-start.2 = (u32[32]{0:T(128)S(1)}, u32[32]{0:T(128)}, u32[]{:S(2)}) copy-start(u32[32]{0:T(128)} %constant.81) | copy-start | bytes 388
  208.5 12.5 %all-to-all-start.1 = ((f32[8,1,16]{2,1,0:T(1,128)}), f32[8,1,16]{2,1,0:T(1,128)S(1)}, u32[]{:S(2)}, u32[]{:S(2)}) async-start(f32[8,1,16]{2,1,0:T(1,128)} %bitcast.25), calls=%async_computation.1 | async-start | bytes 8192 | tf_op jit(solution)/shard_map/all_to_all | solution.py:121
where the time goes:
time: 232 us; the launch traced here: 230 us
  local copies, waits for them, and re-layouts  175 us (75%)
  other arithmetic  19.2 us (8%)
  blocking collectives  14.3 us (6%)
  starting transfers between devices  13.1 us (6%)
  waiting for transfers between devices  7.01 us (3%)
    gather x4, local copies, waits for them, and re-layouts, score(): values = jnp.take(table, index + step_x * lines, axis=0).astype(jnp.float32)  133 us
    reshape x2, local copies, waits for them, and re-layouts, corner_table(): return square.reshape(cells_x * cells_y * (cells_z - 1), 4 * chans)  22 us
    concatenate x1, local copies, waits for them, and re-layouts, corner_table(): square = jnp.concatenate([paired[:, :-1], paired[:, 1:]], axis=3)  10 us
    all_gather x1, blocking collectives, body(): grouped = lax.all_gather(payload, 'tile', axis=0, tiled=True)  7.76 us
    unnamed x1, blocking collectives  6.54 us
    concatenate x1, other arithmetic, corner_table(): square = jnp.concatenate([paired[:, :-1], paired[:, 1:]], axis=3)  6.22 us
    all_to_all x1, starting transfers between devices, body(): lax.all_to_all(partial_value.reshape(slabs, capacity), 'slab', split_axis...  5.99 us
    all_to_all x1, starting transfers between devices, body(): lax.all_to_all(outgoing, 'slab', split_axis=0, concat_axis=0, tiled=True)  5.83 us
  transfers between devices with their start and end apart: 3, of which 2 were waited for; matrix products, arithmetic and copies ran while one was open for 19% of the time, Pallas kernels for 0%

commit v1 on v0

v1 whole, which is shorter than its diff:
```python
import functools

import jax
import jax.numpy as jnp
from jax import lax
from jax.experimental import pallas as pl
from jax.experimental.pallas import tpu as pltpu
from jax.sharding import PartitionSpec as P

SPAN = 32
ROWS = 4
FAR = -1.0e6
MESH = pl.DeviceIdType.MESH


def iota(shape, dim):
    return lax.broadcasted_iota(jnp.int32, shape, dim)


def to_row(col, count):
    eye = iota((count, count), 0) == iota((count, count), 1)
    return jnp.sum(jnp.where(eye, col, 0), axis=0, keepdims=True)


def exchange_kernel(
    slabs, tiles, cap, cells_x,
    counts_ref, base_y_ref, base_z_ref, route_ref, types_ref, offsets_ref,
    incoming_ref,
    gathered, outgoing, tile_send, tile_recv, slab_send, slab_recv,
):
    me_s = lax.axis_index("slab")
    me_t = lax.axis_index("tile")
    poses, atoms = types_ref.shape
    group = tiles * poses
    slots = slabs * cap

    barrier = pltpu.get_barrier_semaphore()
    for i in range(1, tiles):
        pl.semaphore_signal(
            barrier, inc=1, device_id=(me_s, lax.rem(me_t + i, tiles)), device_id_type=MESH
        )

    @pl.loop(1, slabs)
    def _(i):
        pl.semaphore_signal(
            barrier, inc=1, device_id=(lax.rem(me_s + i, slabs), me_t), device_id_type=MESH
        )

    lane = iota((1, atoms), 1)
    for p in range(poses):
        off = offsets_ref[p]
        by = jnp.full((1, atoms), base_y_ref[p], jnp.int32).astype(jnp.float32)
        bz = jnp.full((1, atoms), base_z_ref[p], jnp.int32).astype(jnp.float32)
        kind = jnp.where(lane < counts_ref[p], types_ref[p : p + 1, :], -1)
        gathered[me_t, p : p + 1, 0:atoms] = off[0:1, :] * (cells_x - 1)
        gathered[me_t, p : p + 1, atoms : 2 * atoms] = by + off[1:2, :] * SPAN
        gathered[me_t, p : p + 1, 2 * atoms : 3 * atoms] = bz + off[2:3, :] * SPAN
        gathered[me_t, p : p + 1, 3 * atoms : 4 * atoms] = kind.astype(jnp.float32)

    pl.semaphore_wait(barrier, tiles - 1 + slabs - 1)

    def tile_copy(i, block):
        return pltpu.make_async_remote_copy(
            src_ref=gathered.at[block],
            dst_ref=gathered.at[block],
            send_sem=tile_send.at[i],
            recv_sem=tile_recv.at[i],
            device_id=(me_s, lax.rem(me_t + i, tiles)),
            device_id_type=MESH,
        )

    for i in range(1, tiles):
        tile_copy(i, me_t).start()

    col = route_ref[...]
    row = to_row(col, group)
    before = (iota((group, group), 0) < iota((group, group), 1)) & (col == row)
    rank = jnp.sum(before.astype(jnp.int32), axis=0, keepdims=True)
    hits = iota((slots, group), 0) == row * cap + rank
    pick = hits.astype(jnp.float32).astype(jnp.bfloat16)
    empty = 1.0 - jnp.sum(hits.astype(jnp.float32), axis=1, keepdims=True)

    for i in range(1, tiles):
        tile_copy(i, lax.rem(me_t - i + tiles, tiles)).wait_recv()

    data = gathered[...].reshape(group, ROWS * atoms)
    high = data.astype(jnp.bfloat16)
    rest = data - high.astype(jnp.float32)
    mid = rest.astype(jnp.bfloat16)
    low = (rest - mid.astype(jnp.float32)).astype(jnp.bfloat16)
    dot = functools.partial(jnp.dot, preferred_element_type=jnp.float32)
    routed = (dot(pick, high) + dot(pick, mid)) + dot(pick, low)
    shift = jnp.where(iota((1, ROWS * atoms), 1) // atoms == 1, FAR, 0.0)
    routed = routed + empty * shift
    for s in range(slabs):
        outgoing[s] = routed[s * cap : (s + 1) * cap, :]

    def slab_copy(i, src, dst):
        return pltpu.make_async_remote_copy(
            src_ref=outgoing.at[src],
            dst_ref=incoming_ref.at[dst],
            send_sem=slab_send.at[i],
            recv_sem=slab_recv.at[i],
            device_id=(lax.rem(me_s + i, slabs), me_t),
            device_id_type=MESH,
        )

    @pl.loop(1, slabs)
    def _(i):
        slab_copy(i, lax.rem(me_s + i, slabs), me_s).start()

    incoming_ref[me_s] = outgoing[me_s]
    for i in range(1, tiles):
        tile_copy(i, me_t).wait_send()

    @pl.loop(1, slabs)
    def _(i):
        slab_copy(i, lax.rem(me_s + i, slabs), lax.rem(me_s - i + slabs, slabs)).wait()


def score_kernel(
    cells_x, cells_y, cells_z, chans,
    incoming_ref, gt_ref, table_ref, part_ref,
    lines_of, weights, coefs, sums, plan_v, plan_s, plan_sem,
):
    me_t = lax.axis_index("tile")
    slabs, cap, wide = incoming_ref.shape
    atoms = wide // ROWS
    slots = slabs * cap
    kinds = table_ref.shape[1]
    window = SPAN + 2
    first_row = me_t * cells_y
    first_f = first_row.astype(jnp.float32)

    for r in range(ROWS):
        lines_of[r] = incoming_ref[:, :, r * atoms : (r + 1) * atoms].reshape(slots, atoms)
    ys = lines_of[1]
    zs = lines_of[2]
    y_min = jnp.min(ys, axis=1, keepdims=True)
    y_max = jnp.max(ys, axis=1, keepdims=True)
    z_min = jnp.min(zs, axis=1, keepdims=True)
    start = jnp.minimum((z_min * 0.5).astype(jnp.int32) * 2, cells_z - window)
    near = ((y_max > first_f - 1.0) & (y_min < first_f + cells_y)).astype(jnp.int32)
    near_row = to_row(near, slots)
    up = iota((slots, slots), 0)
    across = iota((slots, slots), 1)
    rank = jnp.sum(jnp.where(across < up, near_row, 0), axis=1, keepdims=True)
    chosen = (rank == across) & (near > 0)
    plan_v[0:1, :] = jnp.sum(jnp.where(chosen, up, 0), axis=0, keepdims=True)
    plan_v[1:2, :] = jnp.sum(jnp.where(chosen, start, 0), axis=0, keepdims=True)
    total = jnp.sum(jnp.broadcast_to(near, (slots, slots)), axis=0, keepdims=True)
    plan_v[2:3, :] = total
    copy = pltpu.make_async_copy(plan_v, plan_s, plan_sem)
    copy.start()
    for t in range(kinds):
        coefs[t] = jnp.broadcast_to(table_ref[:, t : t + 1], (chans, atoms))
    sums[...] = jnp.zeros_like(sums)
    rows_f = (iota((cells_y, atoms), 0) + first_row).astype(jnp.float32)
    cells_f = iota((window, chans, atoms), 0)
    copy.wait()

    @pl.loop(0, plan_s[2, 0])
    def _(i):
        slot = plan_s[0, i]
        z_first = plan_s[1, i]
        x, y, z, kind = (lines_of[r, pl.ds(slot, 1), :] for r in range(ROWS))
        wy = jnp.maximum(1.0 - jnp.abs(y - rows_f), 0.0)
        for cx in range(cells_x):
            wx = jnp.maximum(1.0 - jnp.abs(x - cx), 0.0)
            w = wx * wy
            high = w.astype(jnp.bfloat16)
            low = (w - high.astype(jnp.float32)).astype(jnp.bfloat16)
            weights[cx * cells_y : (cx + 1) * cells_y, 0:atoms] = high
            weights[cx * cells_y : (cx + 1) * cells_y, atoms : 2 * atoms] = low
        lines = pl.ds(pl.multiple_of(z_first * chans, 2 * chans), window * chans)
        mixed = jnp.dot(gt_ref[lines, :], weights[...], preferred_element_type=jnp.float32)
        mixed = (mixed[:, 0:atoms] + mixed[:, atoms:]).reshape(window, chans, atoms)
        wz = jnp.maximum(1.0 - jnp.abs(z[None] - (cells_f + z_first).astype(jnp.float32)), 0.0)
        value = jnp.sum(wz * mixed, axis=0)
        coef = jnp.zeros((chans, atoms), jnp.float32)
        for t in range(kinds):
            coef = jnp.where(kind == t, coefs[t], coef)
        sums[pl.ds(slot, 1), :] = jnp.sum(value * coef, axis=0, keepdims=True)

    part_ref[...] = to_row(jnp.sum(sums[...], axis=1, keepdims=True), slots)


def return_kernel(slabs, tiles, cap, part_ref, route_ref, out_ref, landed, ranks, send, recv):
    me_s = lax.axis_index("slab")
    me_t = lax.axis_index("tile")
    group = route_ref.shape[0]
    poses = group // tiles
    slots = slabs * cap
    devices = slabs * tiles
    me = me_s * tiles + me_t

    barrier = pltpu.get_barrier_semaphore()

    @pl.loop(1, devices)
    def _(i):
        other = lax.rem(me + i, devices)
        pl.semaphore_signal(
            barrier, inc=1, device_id=(other // tiles, lax.rem(other, tiles)), device_id_type=MESH
        )

    col = route_ref[...]
    row = to_row(col, group)
    before = (iota((group, group), 1) < iota((group, group), 0)) & (col == row)
    ranks[...] = jnp.sum(before.astype(jnp.int32), axis=1, keepdims=True)
    pl.semaphore_wait(barrier, devices - 1)

    def copy(i, block):
        other = lax.rem(me + i, devices)
        return pltpu.make_async_remote_copy(
            src_ref=part_ref,
            dst_ref=landed.at[block],
            send_sem=send.at[i],
            recv_sem=recv.at[i],
            device_id=(other // tiles, lax.rem(other, tiles)),
            device_id_type=MESH,
        )

    @pl.loop(1, devices)
    def _(i):
        copy(i, me).start()

    landed[me] = part_ref[...]

    @pl.loop(1, devices)
    def _(i):
        copy(i, lax.rem(me - i + devices, devices)).wait()

    mine = pl.ds(pl.multiple_of(me_t * poses, poses), poses)
    target = route_ref[mine, :]
    rank = ranks[mine, :]
    found = jnp.zeros((poses, slots), jnp.float32)
    for s in range(slabs):
        line = landed[s * tiles]
        for t in range(1, tiles):
            line = line + landed[s * tiles + t]
        found = jnp.where(target == s, line, found)
    found = jnp.where(iota((poses, slots), 1) == me_s * cap + rank, found, 0.0)
    out_ref[...] = jnp.sum(found, axis=1, keepdims=True)


def vmem():
    return pl.BlockSpec(memory_space=pltpu.VMEM)


def smem():
    return pl.BlockSpec(memory_space=pltpu.SMEM)


def body(grid, type_table, counts, types, offsets, route, base_y, base_z):
    slabs = lax.axis_size("slab")
    tiles = lax.axis_size("tile")
    poses, atoms = types.shape
    kinds, chans = type_table.shape
    cells_x, cells_y, wide_z = grid.shape
    cells_z = wide_z // chans
    cap = max(2, 8 * poses // slabs)
    slots = slabs * cap
    devices = slabs * tiles
    dma = pltpu.SemaphoreType.DMA
    incoming = pl.pallas_call(
        functools.partial(exchange_kernel, slabs, tiles, cap, cells_x),
        out_shape=jax.ShapeDtypeStruct((slabs, cap, ROWS * atoms), jnp.float32),
        in_specs=[smem(), smem(), smem(), vmem(), vmem(), vmem()],
        out_specs=vmem(),
        scratch_shapes=[
            pltpu.VMEM((tiles, poses, ROWS * atoms), jnp.float32),
            pltpu.VMEM((slabs, cap, ROWS * atoms), jnp.float32),
            dma((tiles,)), dma((tiles,)), dma((slabs,)), dma((slabs,)),
        ],
        compiler_params=pltpu.CompilerParams(collective_id=0, has_side_effects=True),
        name="exchange",
    )(counts, base_y, base_z, route, types, offsets)
    gt = grid.reshape(cells_x * cells_y, wide_z).T
    part = pl.pallas_call(
        functools.partial(score_kernel, cells_x, cells_y, cells_z, chans),
        out_shape=jax.ShapeDtypeStruct((1, slots), jnp.float32),
        in_specs=[vmem(), vmem(), vmem()],
        out_specs=vmem(),
        scratch_shapes=[
            pltpu.VMEM((ROWS, slots, atoms), jnp.float32),
            pltpu.VMEM((cells_x * cells_y, 2 * atoms), jnp.bfloat16),
            pltpu.VMEM((kinds, chans, atoms), jnp.float32),
            pltpu.VMEM((slots, atoms), jnp.float32),
            pltpu.VMEM((8, slots), jnp.int32),
            pltpu.SMEM((8, slots), jnp.int32),
            dma,
        ],
        name="score",
    )(incoming, gt, type_table.T)
    out = pl.pallas_call(
        functools.partial(return_kernel, slabs, tiles, cap),
        out_shape=jax.ShapeDtypeStruct((poses, 1), jnp.float32),
        in_specs=[vmem(), vmem()],
        out_specs=vmem(),
        scratch_shapes=[
            pltpu.VMEM((devices, 1, slots), jnp.float32),
            pltpu.VMEM((tiles * poses, 1), jnp.int32),
            dma((devices,)), dma((devices,)),
        ],
        compiler_params=pltpu.CompilerParams(collective_id=1, has_side_effects=True),
        name="giveback",
    )(part, route)
    return out[:, 0] / counts.astype(jnp.float32)


def solution(mesh):
    in_specs = (
        P("slab", "tile", None),
        P(),
        P(("slab", "tile")),
        P(("slab", "tile"), None),
        P(("slab", "tile"), None, None),
        P("slab", None),
        P(("slab", "tile")),
        P(("slab", "tile")),
    )
    out_specs = P(("slab", "tile"))
    return jax.shard_map(body, mesh=mesh, in_specs=in_specs, out_specs=out_specs, check_vma=False)
```

time: 232 us -> 53 us (0.23)
  local copies, waits for them, and re-layouts: 175 us -> 4.27 us
  Pallas kernels: 0 us -> 47.5 us
  other arithmetic: 19.2 us -> 1.34 us
  blocking collectives: 14.3 us -> 0 us
  starting transfers between devices: 13.1 us -> 0 us
  waiting for transfers between devices: 7.01 us -> 0 us
    gather x6 -> x0, local copies, waits for them, and re-layouts: 135 us -> none  [the longest x4 133 us: score(): values = jnp.take(table, index + step_x * lines, axis=0).astype(jnp.float32)]
    pallas_call x0 -> x3, Pallas kernels: none -> 47.5 us  [the longest x1 26.1 us: body(): pl.pallas_call(functools.partial(return_kernel, slabs, tiles, cap), out_s...]
    reshape x4 -> x1, local copies, waits for them, and re-layouts: 22.2 us -> 2.3 us  [body(): gt = grid.reshape(cells_x * cells_y, wide_z).T]
    all_to_all x2 -> x0, starting transfers between devices: 11.8 us -> none  [the longest x1 5.99 us: body(): lax.all_to_all(partial_value.reshape(slabs, capacity), 'slab', split_axis...]
    concatenate x3 -> x0, local copies, waits for them, and re-layouts: 11.8 us -> none  [the longest x1 10 us: corner_table(): square = jnp.concatenate([paired[:, :-1], paired[:, 1:]], axis=3)]
    concatenate x4 -> x0, other arithmetic: 8.62 us -> none  [the longest x1 6.22 us: corner_table(): square = jnp.concatenate([paired[:, :-1], paired[:, 1:]], axis=3)]
    all_gather x1 -> x0, blocking collectives: 7.76 us -> none  [body(): grouped = lax.all_gather(payload, 'tile', axis=0, tiled=True)]
    unnamed x1 -> x0, blocking collectives: 6.54 us -> none
  transfers between devices with their start and end apart: 3 -> 0, of which waited for: 2 -> 0; matrix products, arithmetic and copies ran while one was open for 19% -> 0% of each run, Pallas kernels for 0% -> 0%
where the time goes in v1:
time: 53 us; the launch traced here: 53.1 us
  Pallas kernels  47.5 us (90%)
  local copies, waits for them, and re-layouts  4.27 us (8%)
  other arithmetic  1.34 us (3%)
    pallas_call x1, Pallas kernels, body(): pl.pallas_call(functools.partial(return_kernel, slabs, tiles, cap), out_s...  26.1 us
    pallas_call x1, Pallas kernels, body(): pl.pallas_call(functools.partial(exchange_kernel, slabs, tiles, cap, cell...  16.7 us
    pallas_call x1, Pallas kernels, body(): pl.pallas_call(functools.partial(score_kernel, cells_x, cells_y, cells_z,...  4.65 us
    reshape x1, local copies, waits for them, and re-layouts, body(): gt = grid.reshape(cells_x * cells_y, wide_z).T  2.3 us
    unnamed x6, local copies, waits for them, and re-layouts  1.97 us

profile of v1, /device:TPU:0, one launch (start us, length us, event | category | flops | bytes accessed | tf_op | source)
XLA Modules:
  0.0 53.1 jit_solution(3682879582974452281)
XLA Ops:
  0.0 0.0 copy-start
  0.0 1.3 %copy.13.route_ref = s32[64,1]{1,0:T(8,128)} copy(s32[64,1]{0,1:T(1,128)} %param.13) | data formatting | bytes 512 | tf_op args[5]
  1.4 0.0 copy-done
  1.4 0.6 %copy.14.offsets_ref = f32[16,3,128]{2,1,0:T(4,128)} copy(f32[16,3,128]{2,0,1:T(8,128)S(1)} %copy-done) | data formatting | bytes 49152 | tf_op args[4]
  2.0 16.7 %exchange.1.incoming_ref = f32[8,16,512]{2,1,0:T(8,128)} custom-call(s32[16]{0:T(128)} %counts_ref.1, s32[16]{0:T(128)} %base_y_ref.1, s32[16]{0:T(128)} %base_z_ref.1, s32[64,1]{1,0:T(8,128)} %copy.13.route_ref, s32[16,128]{1,0:T(8,128)} %types_ref.1, f32[16,3,128]{2,1,0:T(4,128)} %copy.14.offsets_ref), custom_call_target="tpu_custom_call" | custom-call | tf_op jit(solution)/shard_map/exchange/pallas_call | solution.py:265
  18.7 2.3 %copy.15 = bf16[512,1024]{0,1:T(8,128)(2,1)} copy(bf16[512,1024]{1,0:T(8,128)(2,1)} %bitcast.4) | data formatting | bytes 2097152 | tf_op jit(solution)/shard_map/reshape | solution.py:278
  21.0 4.7 %score.1.part_ref = f32[1,128]{1,0:T(1,128)} custom-call(f32[8,16,512]{2,1,0:T(8,128)} %exchange.1.incoming_ref, bf16[1024,512]{1,0:T(8,128)(2,1)} %bitcast.3, f32[8,16]{1,0:T(8,128)} %bitcast.5), custom_call_target="tpu_custom_call" | custom-call | tf_op jit(solution)/shard_map/score/pallas_call | solution.py:279
  25.6 26.1 %giveback.1 = f32[16,1]{1,0:T(8,128)} custom-call(f32[1,128]{1,0:T(1,128)} %score.1.part_ref, s32[64,1]{1,0:T(8,128)} %copy.13.route_ref), custom_call_target="tpu_custom_call" | custom-call | tf_op jit(solution)/shard_map/giveback/pallas_call | solution.py:295
  51.8 0.0 copy-start.1
  51.8 0.8 %reduce = f32[16]{0:T(128)S(1)} reduce(f32[16,1]{1,0:T(8,128)} %giveback.1, f32[]{:T(128)} %constant.5), dimensions={1}, to_apply=%pallas_call.11.reduce_sub_computation | reduce | bytes 132 | tf_op jit(solution)/shard_map/giveback/pallas_call | solution.py:295
  52.6 0.0 copy-done.1
  52.6 0.5 convert_divide_fusion
Async XLA Ops:
  0.0 1.4 %copy-start = (f32[16,3,128]{2,0,1:T(8,128)S(1)}, f32[16,3,128]{2,0,1:T(8,128)}, u32[]{:S(2)}) copy-start(f32[16,3,128]{2,0,1:T(8,128)} %param.12) | copy-start | bytes 73732
  51.8 0.8 %copy-start.1 = (s32[16]{0:T(128)S(1)}, s32[16]{0:T(128)}, u32[]{:S(2)}) copy-start(s32[16]{0:T(128)} %counts_ref.1) | copy-start | bytes 196
